TPU v7x, 128 devices: a whole 4x4x4 slice. The times are simulated.
128 devices in a mesh: row: 8 (over z, core), col: 16 (over x, y).
Axes of the slice: x: 4, y: 4, z: 4, core: 2. Of those that a mesh axis runs over, the one named last changes fastest.
Arguments:
- tile_data: bfloat16 [8, 16, 256, 128, 128], P('row', 'col')
- tile_rows: int32 [8, 16, 256], P('row', 'col'), may hold values from 0 to 15, as said below
- tile_cols: int32 [8, 16, 256], P('row', 'col'), may hold values from 0 to 31
- tile_count: int32 [8, 16], P('row', 'col'), may hold values from 32 to 256, as said below
- sketch: bfloat16 [65536, 256], P('col')
Outputs:
- range_one: float32 [16384, 256], P(('row', 'col'))
- basis: float32 [16384, 256], P(('row', 'col'))
Inputs may be any that keep to these rules, and one draw needn't show every extreme that they name: On each device the pairs (tile_rows, tile_cols) are distinct. A device's live tiles are its first tile_count tiles; the rest are padding.
All inputs are finite; a program needn't handle non-finite values.
Results may differ from a plain program's by a relative error of at most 0.0028.
Values may be sent and summed in bfloat16 or wider, within the bound.
A program may use at most 128 MiB of HBM per device.

v0:
```python
import math

import jax
import jax.numpy as jnp
from jax import lax
from jax.sharding import PartitionSpec as P

RB_G = 16
CB_G = 32


def tile_product(tiles, out_index, in_index, count, operand, n_out, flip):
    total_tiles = tiles.shape[0]
    width = min(64, total_tiles)
    blocks = total_tiles // width
    form = "tba,tbk->tak" if flip else "tab,tbk->tak"
    targets = jnp.arange(n_out, dtype=jnp.int32)

    def step(number, total):
        start = number * width
        block = lax.dynamic_slice_in_dim(tiles, start, width, 0)
        target = lax.dynamic_slice_in_dim(out_index, start, width, 0)
        source = lax.dynamic_slice_in_dim(in_index, start, width, 0)
        gathered = jnp.take(operand, source, axis=0)
        product = jnp.einsum(form, block, gathered, preferred_element_type=jnp.float32)
        weight = (start + jnp.arange(width, dtype=jnp.int32) < count).astype(jnp.float32)
        select = (target[None, :] == targets[:, None]).astype(jnp.float32) * weight[None, :]
        return total + jnp.einsum("nt,tak->nak", select, product, precision=lax.Precision.HIGHEST)

    start_total = jnp.zeros((n_out, tiles.shape[1], operand.shape[2]), jnp.float32)
    return lax.fori_loop(0, blocks, step, start_total)


def gram_of(values):
    return jnp.dot(values.T, values, precision=lax.Precision.HIGHEST)


def orthonormal(values, gram):
    lower = jnp.linalg.cholesky(gram)
    inverse = lax.linalg.triangular_solve(
        lower, jnp.eye(gram.shape[0], dtype=jnp.float32), left_side=True, lower=True
    )
    return jnp.dot(values, inverse.T, precision=lax.Precision.HIGHEST)


def body(tile_data, tile_rows, tile_cols, tile_count, sketch):
    tiles = tile_data[0, 0]
    row_index = tile_rows[0, 0]
    col_index = tile_cols[0, 0]
    count = tile_count[0, 0]
    edge = tiles.shape[1]
    width_k = sketch.shape[1]
    row_blocks = RB_G
    col_blocks = CB_G
    rows_total = row_blocks * edge * lax.axis_size("row")
    scale_rows = math.sqrt(rows_total)
    omega = sketch.reshape(col_blocks, edge, width_k)
    first = tile_product(tiles, row_index, col_index, count, omega, row_blocks, False)
    first = first.reshape(row_blocks * edge, width_k)
    share = lax.psum_scatter(first, "col", scatter_dimension=0, tiled=True)
    gram = lax.psum(gram_of(share), ("row", "col"))
    share_float = orthonormal(share, gram)
    range_one = share_float * scale_rows
    ortho_one = lax.all_gather(share_float.astype(jnp.bfloat16), "col", axis=0, tiled=True)
    cross = tile_product(
        tiles,
        col_index,
        row_index,
        count,
        ortho_one.reshape(row_blocks, edge, width_k),
        col_blocks,
        True,
    )
    cross = cross.reshape(col_blocks * edge, width_k)
    cross_full = lax.psum(cross, "row").astype(jnp.bfloat16)
    second = tile_product(
        tiles,
        row_index,
        col_index,
        count,
        cross_full.reshape(col_blocks, edge, width_k),
        row_blocks,
        False,
    )
    second = second.reshape(row_blocks * edge, width_k)
    second_share = lax.psum_scatter(second, "col", scatter_dimension=0, tiled=True)
    gram_two = lax.psum(gram_of(second_share), ("row", "col"))
    return (range_one, orthonormal(second_share, gram_two) * scale_rows)


def solution(mesh):
    placed = (
        P("row", "col", None, None, None),
        P("row", "col", None),
        P("row", "col", None),
        P("row", "col"),
        P("col", None),
    )
    return jax.shard_map(
        body,
        mesh=mesh,
        in_specs=placed,
        out_specs=(P(("row", "col"), None), P(("row", "col"), None)),
        check_vma=False,
    )
```

profile of v0, /device:TPU:1, one launch (start us, length us, event | category | flops | bytes accessed | tf_op | source)
XLA Modules:
  0.0 1008.3 jit_solution(9509779898938433032)
XLA Ops:
  7.2 102.7 %while.46 = (s32[]{:T(128)}, f32[16,128,256]{2,0,1:T(8,128)S(1)}, s32[256]{0:T(256)}, s32[]{:T(128)}, bf16[256,128,128]{2,1,0:T(8,128)(2,1)}, /*index=5*/s32[256...) while((s32[]{:T(128)}, f32[16,128,256]{2,0,1:T(8,128)S(1)}, ...), condition=%wide.region_1.3_spmd.clone, body=%wide.region_0.2_spmd.clone.sunk | while | flops 942673472 | bytes 35662420 | solution.py:31
  8.7 4.4 gather_fusion
  13.0 7.4 fusion.123
  20.5 12.4 %select_add_fusion.6 = f32[16,128,256]{2,0,1:T(8,128)S(1)} fusion(f32[16,128,256]{2,0,1:T(8,128)S(1)} %get-tuple-element.823, f32[64,128,256]{2,1,0:T(8,128)} %fusion.123, pred[]{:T(512)S(6)} %compare.38, f32[64]{0:T(128)S(1)} %get-tuple-element.778, s32[64]{0:T(128)S(1)} %dynamic_slice.91), kind=kOutput, calls=%fused_computation.37.clone.1 | convolution fusion | flops 403703808 | bytes 12583425 | tf_op jit(solution)/shard_map/while/body/eval_jaxpr/nt,tak->nak/dot_general | solution.py:28
  34.3 4.4 gather_fusion
  38.7 7.4 fusion.123
  46.2 12.4 %select_add_fusion.6 = f32[16,128,256]{2,0,1:T(8,128)S(1)} fusion(f32[16,128,256]{2,0,1:T(8,128)S(1)} %get-tuple-element.823, f32[64,128,256]{2,1,0:T(8,128)} %fusion.123, pred[]{:T(512)S(6)} %compare.38, f32[64]{0:T(128)S(1)} %get-tuple-element.778, s32[64]{0:T(128)S(1)} %dynamic_slice.91), kind=kOutput, calls=%fused_computation.37.clone.1 | convolution fusion | flops 403703808 | bytes 12583425 | tf_op jit(solution)/shard_map/while/body/eval_jaxpr/nt,tak->nak/dot_general | solution.py:28
  60.0 4.4 gather_fusion
  64.4 7.4 fusion.123
  71.9 12.4 %select_add_fusion.6 = f32[16,128,256]{2,0,1:T(8,128)S(1)} fusion(f32[16,128,256]{2,0,1:T(8,128)S(1)} %get-tuple-element.823, f32[64,128,256]{2,1,0:T(8,128)} %fusion.123, pred[]{:T(512)S(6)} %compare.38, f32[64]{0:T(128)S(1)} %get-tuple-element.778, s32[64]{0:T(128)S(1)} %dynamic_slice.91), kind=kOutput, calls=%fused_computation.37.clone.1 | convolution fusion | flops 403703808 | bytes 12583425 | tf_op jit(solution)/shard_map/while/body/eval_jaxpr/nt,tak->nak/dot_general | solution.py:28
  85.7 4.4 gather_fusion
  90.1 7.4 fusion.123
  97.6 12.4 %select_add_fusion.6 = f32[16,128,256]{2,0,1:T(8,128)S(1)} fusion(f32[16,128,256]{2,0,1:T(8,128)S(1)} %get-tuple-element.823, f32[64,128,256]{2,1,0:T(8,128)} %fusion.123, pred[]{:T(512)S(6)} %compare.38, f32[64]{0:T(128)S(1)} %get-tuple-element.778, s32[64]{0:T(128)S(1)} %dynamic_slice.91), kind=kOutput, calls=%fused_computation.37.clone.1 | convolution fusion | flops 403703808 | bytes 12583425 | tf_op jit(solution)/shard_map/while/body/eval_jaxpr/nt,tak->nak/dot_general | solution.py:28
  110.0 2.6 copy.11
  112.6 76.8 %reduce-scatter.3.cloned.1.call-done = f32[128,256]{1,0:T(8,128)} async-done(((f32[2048,256]{1,0:T(8,128)}), f32[128,256]{1,0:T(8,128)}) %reduce-scatter.3.cloned.1.call-update) | async-done | bytes 131088 | tf_op jit(solution)/shard_map/reduce_scatter | solution.py:60
  189.4 2.2 fusion.86
  191.9 146.5 %all-reduce.5.cloned.1.call-done = f32[256,256]{0,1:T(8,128)} async-done(((f32[256,256]{0,1:T(8,128)}), f32[256,256]{0,1:T(8,128)}) %all-reduce.5.cloned.1.call-update) | async-done | bytes 262160 | tf_op jit(solution)/shard_map/psum | solution.py:61
  340.5 11.7 %cholesky.130 = f32[128,128]{1,0:T(8,128)S(1)} custom-call(f32[128,128]{1,0:T(8,128)S(1)} %cholesky.194), custom_call_target="Cholesky" | custom-call | tf_op jit(solution)/shard_map/jit(cholesky)/cholesky | solution.py:39
  352.2 9.8 custom-call.16
  362.6 11.7 %cholesky.147 = f32[128,128]{1,0:T(8,128)S(1)} custom-call(f32[128,128]{1,0:T(8,128)S(1)} %convolution_subtract_fusion.3), custom_call_target="Cholesky" | custom-call | tf_op jit(solution)/shard_map/jit(cholesky)/cholesky | solution.py:39
  376.5 4.3 while.49
  377.3 1.4 bitcast_dynamic-update-slice_fusion.4
  379.4 1.4 bitcast_dynamic-update-slice_fusion.4
  380.8 19.7 %custom-call.17 = f32[2,128,128]{1,2,0:T(8,128)S(1)} custom-call(f32[2,128,128]{2,1,0:T(8,128)S(1)} %get-tuple-element.517), custom_call_target="InvertDiagBlocksLowerTriangular" | custom-call | tf_op jit(solution)/shard_map/triangular_solve/custom-call.0 | solution.py:40
  402.6 38.1 %all-gather.2.cloned.1.call-done = bf16[2048,256]{1,0:T(8,128)(2,1)} async-done(((bf16[128,256]{1,0:T(8,128)(2,1)}), bf16[2048,256]{1,0:T(8,128)(2,1)}) %all-gather.2.cloned.1.call-update) | async-done | bytes 1048592 | tf_op jit(solution)/shard_map/all_gather | solution.py:64
  440.7 107.3 %while.47 = (s32[]{:T(128)}, f32[32,128,256]{2,0,1:T(8,128)}, s32[256]{0:T(256)S(1)}, s32[]{:T(128)}, bf16[256,128,128]{2,1,0:T(8,128)(2,1)}, /*index=5*/s32[256...) while((s32[]{:T(128)}, f32[32,128,256]{2,0,1:T(8,128)}, ...), condition=%wide.region_9.13_spmd.clone, body=%wide.region_8.12_spmd.clone.sunk | while | flops 1346377216 | bytes 39852600 | solution.py:31
  441.4 4.0 gather_fusion.1
  445.4 7.4 fusion.128
  452.9 14.1 %select_add_fusion.7 = f32[32,128,256]{2,0,1:T(8,128)} fusion(f32[32,128,256]{2,0,1:T(8,128)} %get-tuple-element.871, f32[64,128,256]{2,1,0:T(8,128)} %fusion.128, pred[]{:T(512)S(6)} %compare.39, f32[64]{0:T(128)S(1)} %get-tuple-element.788, s32[64]{0:T(128)S(1)} %dynamic_slice.93), kind=kOutput, calls=%fused_computation.12.clone.1 | convolution fusion | flops 807407616 | bytes 16777728 | tf_op jit(solution)/shard_map/while/body/eval_jaxpr/nt,tak->nak/dot_general | solution.py:28
  467.7 4.0 gather_fusion.1
  471.7 7.4 fusion.128
  479.2 14.8 %select_add_fusion.7 = f32[32,128,256]{2,0,1:T(8,128)} fusion(f32[32,128,256]{2,0,1:T(8,128)} %get-tuple-element.871, f32[64,128,256]{2,1,0:T(8,128)} %fusion.128, pred[]{:T(512)S(6)} %compare.39, f32[64]{0:T(128)S(1)} %get-tuple-element.788, s32[64]{0:T(128)S(1)} %dynamic_slice.93), kind=kOutput, calls=%fused_computation.12.clone.1 | convolution fusion | flops 807407616 | bytes 16777728 | tf_op jit(solution)/shard_map/while/body/eval_jaxpr/nt,tak->nak/dot_general | solution.py:28
  494.7 4.0 gather_fusion.1
  498.7 7.4 fusion.128
  506.2 14.8 %select_add_fusion.7 = f32[32,128,256]{2,0,1:T(8,128)} fusion(f32[32,128,256]{2,0,1:T(8,128)} %get-tuple-element.871, f32[64,128,256]{2,1,0:T(8,128)} %fusion.128, pred[]{:T(512)S(6)} %compare.39, f32[64]{0:T(128)S(1)} %get-tuple-element.788, s32[64]{0:T(128)S(1)} %dynamic_slice.93), kind=kOutput, calls=%fused_computation.12.clone.1 | convolution fusion | flops 807407616 | bytes 16777728 | tf_op jit(solution)/shard_map/while/body/eval_jaxpr/nt,tak->nak/dot_general | solution.py:28
  521.7 4.0 gather_fusion.1
  525.7 7.4 fusion.128
  533.2 14.8 %select_add_fusion.7 = f32[32,128,256]{2,0,1:T(8,128)} fusion(f32[32,128,256]{2,0,1:T(8,128)} %get-tuple-element.871, f32[64,128,256]{2,1,0:T(8,128)} %fusion.128, pred[]{:T(512)S(6)} %compare.39, f32[64]{0:T(128)S(1)} %get-tuple-element.788, s32[64]{0:T(128)S(1)} %dynamic_slice.93), kind=kOutput, calls=%fused_computation.12.clone.1 | convolution fusion | flops 807407616 | bytes 16777728 | tf_op jit(solution)/shard_map/while/body/eval_jaxpr/nt,tak->nak/dot_general | solution.py:28
  548.0 6.5 copy.14
  554.5 58.1 %all-reduce.8 = bf16[4096,256]{1,0:T(8,128)(2,1)S(1)} all-reduce(f32[4096,256]{1,0:T(8,128)} %bitcast.97), channel_id=1, replica_groups=mesh['row'=8,'col'=16] {'row'}, use_global_device_ids=true, to_apply=%region_10.14 | all-reduce | flops 1048576 | bytes 6291456 | tf_op jit(solution)/shard_map/psum | solution.py:75
  612.6 98.0 %while.48 = (s32[]{:T(128)}, f32[16,128,256]{2,0,1:T(8,128)}, s32[256]{0:T(256)S(1)}, s32[]{:T(128)}, bf16[256,128,128]{2,1,0:T(8,128)(2,1)}, /*index=5*/s32[256...) while((s32[]{:T(128)}, f32[16,128,256]{2,0,1:T(8,128)}, ...), condition=%wide.region_12.16_spmd.clone, body=%wide.region_11.15_spmd.clone.sunk | while | flops 942673472 | bytes 35658296 | solution.py:31
  613.3 2.8 gather_fusion.2
  616.1 7.4 fusion.133
  623.6 13.3 %select_add_fusion.8 = f32[16,128,256]{2,0,1:T(8,128)} fusion(f32[16,128,256]{2,0,1:T(8,128)} %get-tuple-element.904, f32[64,128,256]{2,1,0:T(8,128)} %fusion.133, pred[]{:T(512)S(6)} %compare.40, f32[64]{0:T(128)S(1)} %get-tuple-element.798, s32[64]{0:T(128)S(1)} %dynamic_slice.95), kind=kOutput, calls=%fused_computation.58.clone.1 | convolution fusion | flops 403703808 | bytes 12583425 | tf_op jit(solution)/shard_map/while/body/eval_jaxpr/nt,tak->nak/dot_general | solution.py:28
  637.6 2.8 gather_fusion.2
  640.4 7.4 fusion.133
  647.9 13.6 %select_add_fusion.8 = f32[16,128,256]{2,0,1:T(8,128)} fusion(f32[16,128,256]{2,0,1:T(8,128)} %get-tuple-element.904, f32[64,128,256]{2,1,0:T(8,128)} %fusion.133, pred[]{:T(512)S(6)} %compare.40, f32[64]{0:T(128)S(1)} %get-tuple-element.798, s32[64]{0:T(128)S(1)} %dynamic_slice.95), kind=kOutput, calls=%fused_computation.58.clone.1 | convolution fusion | flops 403703808 | bytes 12583425 | tf_op jit(solution)/shard_map/while/body/eval_jaxpr/nt,tak->nak/dot_general | solution.py:28
  662.2 2.8 gather_fusion.2
  665.0 7.4 fusion.133
  672.4 13.6 %select_add_fusion.8 = f32[16,128,256]{2,0,1:T(8,128)} fusion(f32[16,128,256]{2,0,1:T(8,128)} %get-tuple-element.904, f32[64,128,256]{2,1,0:T(8,128)} %fusion.133, pred[]{:T(512)S(6)} %compare.40, f32[64]{0:T(128)S(1)} %get-tuple-element.798, s32[64]{0:T(128)S(1)} %dynamic_slice.95), kind=kOutput, calls=%fused_computation.58.clone.1 | convolution fusion | flops 403703808 | bytes 12583425 | tf_op jit(solution)/shard_map/while/body/eval_jaxpr/nt,tak->nak/dot_general | solution.py:28
  686.8 2.8 gather_fusion.2
  689.6 7.4 fusion.133
  697.0 13.6 %select_add_fusion.8 = f32[16,128,256]{2,0,1:T(8,128)} fusion(f32[16,128,256]{2,0,1:T(8,128)} %get-tuple-element.904, f32[64,128,256]{2,1,0:T(8,128)} %fusion.133, pred[]{:T(512)S(6)} %compare.40, f32[64]{0:T(128)S(1)} %get-tuple-element.798, s32[64]{0:T(128)S(1)} %dynamic_slice.95), kind=kOutput, calls=%fused_computation.58.clone.1 | convolution fusion | flops 403703808 | bytes 12583425 | tf_op jit(solution)/shard_map/while/body/eval_jaxpr/nt,tak->nak/dot_general | solution.py:28
  710.6 4.2 copy.15
  715.0 73.1 %reduce-scatter.5.cloned.1.call-done = f32[128,256]{1,0:T(8,128)} async-done(((f32[2048,256]{1,0:T(8,128)}), f32[128,256]{1,0:T(8,128)}) %reduce-scatter.5.cloned.1.call-update) | async-done | bytes 131088 | tf_op jit(solution)/shard_map/reduce_scatter | solution.py:86
  788.1 2.2 fusion.87
  790.3 146.6 %all-reduce.7.cloned.1.call-done = f32[256,256]{0,1:T(8,128)} async-done(((f32[256,256]{0,1:T(8,128)}), f32[256,256]{0,1:T(8,128)}) %all-reduce.7.cloned.1.call-update) | async-done | bytes 262160 | tf_op jit(solution)/shard_map/psum | solution.py:87
  939.0 11.7 %cholesky.164 = f32[128,128]{1,0:T(8,128)S(1)} custom-call(f32[128,128]{1,0:T(8,128)S(1)} %cholesky.197), custom_call_target="Cholesky" | custom-call | tf_op jit(solution)/shard_map/jit(cholesky)/cholesky | solution.py:39
  950.7 9.8 custom-call.18
  961.0 11.7 %cholesky.181 = f32[128,128]{1,0:T(8,128)S(1)} custom-call(f32[128,128]{1,0:T(8,128)S(1)} %convolution_subtract_fusion.2), custom_call_target="Cholesky" | custom-call | tf_op jit(solution)/shard_map/jit(cholesky)/cholesky | solution.py:39
  975.5 4.3 while.50
  976.4 1.4 bitcast_dynamic-update-slice_fusion.5
  978.4 1.4 bitcast_dynamic-update-slice_fusion.5
  979.9 19.7 %custom-call.19 = f32[2,128,128]{1,2,0:T(8,128)S(1)} custom-call(f32[2,128,128]{2,1,0:T(8,128)S(1)} %get-tuple-element.518), custom_call_target="InvertDiagBlocksLowerTriangular" | custom-call | tf_op jit(solution)/shard_map/triangular_solve/custom-call.0 | solution.py:40
  (107 shorter events, 26.9 us)
Async XLA Ops:
  7.2 182.3 %reduce-scatter.3.cloned.1.call-start = ((), (), s32[]{:S(2)}) async-start(), calls=%async_computation.2 | async-start | bytes 2228224 | tf_op jit(solution)/shard_map/reduce_scatter | solution.py:60
  13.0 7.4 copy-start.3
  38.7 7.4 copy-start.3
  64.4 7.4 copy-start.3
  90.1 7.4 copy-start.3
  112.5 328.1 %copy-start.2 = (s32[256]{0:T(256)S(1)}, s32[256]{0:T(256)}, u32[]{:S(2)}) copy-start(s32[256]{0:T(256)} %get-tuple-element.964) | copy-start | bytes 3076
  112.5 328.1 %copy-start.4 = (s32[256]{0:T(256)S(1)}, s32[256]{0:T(256)}, u32[]{:S(2)}) copy-start(s32[256]{0:T(256)} %get-tuple-element.966) | copy-start | bytes 3076
  112.6 225.8 %all-reduce.5.cloned.1.call-start = ((), (), s32[]{:S(2)}) async-start(), calls=%async_computation.3 | async-start | bytes 524288 | tf_op jit(solution)/shard_map/psum | solution.py:61
  189.4 212.0 %copy-start = (f32[128,256]{1,0:T(8,128)S(1)}, f32[128,256]{1,0:T(8,128)}, u32[]{:S(2)}) copy-start(f32[128,256]{1,0:T(8,128)} %reduce-scatter.3.cloned.1.call-done) | copy-start | bytes 393220
  191.6 249.0 %all-gather.2.cloned.1.call-start = ((), (), s32[]{:S(2)}) async-start(), calls=%async_computation.4 | async-start | bytes 1114112 | tf_op jit(solution)/shard_map/all_gather | solution.py:64
  402.6 385.6 %reduce-scatter.5.cloned.1.call-start = ((), (), s32[]{:S(2)}) async-start(), calls=%async_computation.5 | async-start | bytes 2228224 | tf_op jit(solution)/shard_map/reduce_scatter | solution.py:86
  714.8 222.1 %all-reduce.7.cloned.1.call-start = ((), (), s32[]{:S(2)}) async-start(), calls=%async_computation.6 | async-start | bytes 524288 | tf_op jit(solution)/shard_map/psum | solution.py:87
  788.1 212.3 %copy-start.1 = (f32[128,256]{1,0:T(8,128)S(1)}, f32[128,256]{1,0:T(8,128)}, u32[]{:S(2)}) copy-start(f32[128,256]{1,0:T(8,128)} %reduce-scatter.5.cloned.1.call-done) | copy-start | bytes 393220
Sparse Core Ops, SparseCore 0:
  112.7 76.6 reduce-scatter.2
  194.2 144.1 all-reduce.4
  402.7 37.9 all-gather.1
  714.9 73.1 reduce-scatter.4
  792.7 144.1 all-reduce.6
where the time goes:
time: 1020 us; the launch traced here: 1010 us
  waiting for transfers between devices  481 us (47%)
  matrix products  260 us (25%)
  other arithmetic  122 us (12%)
  local copies, waits for them, and re-layouts  69.3 us (7%)
  blocking collectives  58.1 us (6%)
  between operations  17 us (2%)
    dot_general x12, matrix products, step(): jnp.einsum('nt,tak->nak', select, product, precision=lax.Precision.HIGHEST)  162 us
    psum x1, waiting for transfers between devices, body(): gram_two = lax.psum(gram_of(second_share), ('row', 'col'))  147 us
    psum x1, waiting for transfers between devices, body(): gram = lax.psum(gram_of(share), ('row', 'col'))  147 us
    dot_general x12, matrix products, step(): jnp.einsum(form, block, gathered, preferred_element_type=jnp.float32)  88.6 us
    reduce_scatter x1, waiting for transfers between devices, body(): share = lax.psum_scatter(first, 'col', scatter_dimension=0, tiled=True)  76.8 us
    reduce_scatter x1, waiting for transfers between devices, body(): lax.psum_scatter(second, 'col', scatter_dimension=0, tiled=True)  73.1 us
    another operation x13, other arithmetic, orthonormal(): lower = jnp.linalg.cholesky(gram)  68.7 us
    psum x1, blocking collectives, body(): cross_full = lax.psum(cross, 'row').astype(jnp.bfloat16)  58.1 us
  transfers between devices with their start and end apart: 5, of which 5 were waited for; matrix products, arithmetic and copies ran while one was open for 0% of the time, Pallas kernels for 0%

commit v1 on v0

v1 whole, which is shorter than its diff:
```python
import math

import jax
import jax.numpy as jnp
from jax import lax
from jax.experimental import pallas as pl
from jax.experimental.pallas import tpu as pltpu
from jax.sharding import PartitionSpec as P

MESH = pl.DeviceIdType.MESH
F32, BF16 = jnp.float32, jnp.bfloat16
HI = lax.Precision.HIGHEST
TILE, K, RB, CB = 128, 256, 16, 32
ROWS_DEV, COLS_DEV = RB * TILE, CB * TILE
COPIES = 176


def flip(c, e):
    if e == 1:
        return c + 1 - 2 * (c % 2)
    if e == 2:
        return (c + 2) % 4
    return 3 - c


ORDERS = ((0, 1, 3), (0, 3, 1), (1, 1, 3), (1, 3, 1))


class Net:
    def __init__(self, send, recv):
        self.send, self.recv, self.count = send, recv, 0
        self.open = []
        r, c = lax.axis_index("row"), lax.axis_index("col")
        self.z, self.core, self.x, self.y = r // 2, r % 2, c // 4, c % 4
        self.row, self.col = r, c

    def to(self, x=None, y=None, z=None, core=None):
        x = self.x if x is None else x
        y = self.y if y is None else y
        z = self.z if z is None else z
        core = self.core if core is None else core
        return (z * 2 + core, x * 4 + y)

    def start(self, src, dst, device):
        n = self.count
        self.count += 1
        copy = pltpu.make_async_remote_copy(
            src_ref=src, dst_ref=dst, send_sem=self.send.at[n], recv_sem=self.recv.at[n],
            device_id=device, device_id_type=MESH,
        )
        copy.start()
        self.open.append(copy)
        return copy

    def close(self):
        for copy in self.open:
            copy.wait_send()
        self.open = []


def at2(ref, axis, a, b, *rest):
    return ref.at[(a, b, *rest)] if axis == 0 else ref.at[(b, a, *rest)]


ALL = slice(None)


def reduce_scatter(net, part, r0, r1, r2, r3):
    pos = (net.x, net.y)

    def peer(axis, e):
        return net.to(x=flip(net.x, e)) if axis == 0 else net.to(y=flip(net.y, e))

    def add(axis, a, b, q, value):
        ref = at2(part, axis, a, b, q)
        ref[...] = ref[...] + value

    copies = []
    for q, (axis, e, g) in enumerate(ORDERS):
        c = pos[axis]
        copies.append([
            net.start(at2(part, axis, flip(c, e), ALL, q), r0.at[q, 0], peer(axis, e)),
            net.start(at2(part, axis, flip(c, 2), ALL, q), r0.at[q, 1], peer(axis, e)),
        ])
    for q, (axis, e, g) in enumerate(ORDERS):
        c = pos[axis]
        copies[q][1].wait_recv()
        add(axis, flip(c, g), ALL, q, r0[q, 1])
        copies[q].append(net.start(at2(part, axis, flip(c, g), ALL, q), r1.at[q], peer(axis, g)))
        copies[q][0].wait_recv()
        add(axis, c, ALL, q, r0[q, 0])
    for q, (axis, e, g) in enumerate(ORDERS):
        c, d, other = pos[axis], pos[1 - axis], 1 - axis
        copies[q][2].wait_recv()
        add(axis, c, ALL, q, r1[q])
        copies[q].append(net.start(at2(part, other, flip(d, e), c, q), r2.at[q, 0], peer(other, e)))
        copies[q].append(net.start(at2(part, other, flip(d, 2), c, q), r2.at[q, 1], peer(other, e)))
    for q, (axis, e, g) in enumerate(ORDERS):
        c, d, other = pos[axis], pos[1 - axis], 1 - axis
        copies[q][4].wait_recv()
        add(axis, c, flip(d, g), q, r2[q, 1])
        copies[q].append(net.start(at2(part, other, flip(d, g), c, q), r3.at[q], peer(other, g)))
        copies[q][3].wait_recv()
        add(axis, c, d, q, r2[q, 0])
    for q, (axis, e, g) in enumerate(ORDERS):
        copies[q][5].wait_recv()
        add(axis, pos[axis], pos[1 - axis], q, r3[q])


class Gather:
    def __init__(self, net, buf):
        self.net, self.buf, self.step, self.flying = net, buf, 0, []

    def advance(self):
        net, buf, t = self.net, self.buf, self.step
        for copy in self.flying:
            copy.wait_recv()
        self.flying = []
        self.step += 1
        if t == 4:
            return
        pos = (net.x, net.y)
        for q, (axis, e, g) in enumerate(ORDERS):
            c, d, other = pos[axis], pos[1 - axis], 1 - axis
            link = (axis, e) if t == 0 else (axis, g) if t == 1 else (other, e) if t == 2 else (other, g)
            dev = net.to(x=flip(net.x, link[1])) if link[0] == 0 else net.to(y=flip(net.y, link[1]))
            if t == 0:
                parts = [(c, d)]
            elif t == 1:
                parts = [(c, d), (flip(c, e), d)]
            elif t == 2:
                parts = [(ALL, d)]
            else:
                parts = [(ALL, d), (ALL, flip(d, e))]
            for a, b in parts:
                ref = at2(buf, axis, a, b, q)
                self.flying.append(net.start(ref, ref, dev))


class GramSum:
    def __init__(self, net, g, h, r0, r1, r2, ga, out):
        self.net, self.g, self.h, self.r0, self.r1, self.r2, self.ga, self.out = net, g, h, r0, r1, r2, ga, out
        self.phase, self.flying = 0, []

    def advance(self):
        net, half = self.net, K // 2
        for copy in self.flying:
            copy.wait_recv()
        self.flying = []
        phase = self.phase
        self.phase += 1
        other = net.to(core=1 - net.core)
        mine = pl.ds(pl.multiple_of(net.core * half, half), half)
        theirs = pl.ds(pl.multiple_of((1 - net.core) * half, half), half)
        if phase == 0:
            self.flying.append(net.start(self.g.at[theirs], self.r0, other))
        elif phase == 1:
            self.h[...] = (self.g[mine, :] + self.r0[...]).reshape(16, 8, K)
            for n in range(1, 16):
                j = (net.col + n) % 16
                self.flying.append(net.start(self.h.at[j], self.r1.at[n], (net.row, j)))
            self.r1[0] = self.h[net.col]
        elif phase == 2:
            self.r2[net.z] = jnp.sum(self.r1[...], axis=0)
            for n in range(1, 4):
                z = (net.z + n) % 4
                self.flying.append(net.start(self.r2.at[net.z], self.r2.at[net.z], net.to(z=z)))
        elif phase == 3:
            self.ga[net.col] = jnp.sum(self.r2[...], axis=0)
            for n in range(1, 16):
                j = (net.col + n) % 16
                self.flying.append(net.start(self.ga.at[net.col], self.ga.at[net.col], (net.row, j)))
        elif phase == 4:
            self.out[net.core] = self.ga[...]
            self.flying.append(net.start(self.ga, self.out.at[net.core], other))


class Factor:
    B = 32

    def __init__(self, g, w):
        self.g, self.w, self.block = g, w, 0

    def begin(self):
        r = lax.broadcasted_iota(jnp.int32, (K, K), 0)
        c = lax.broadcasted_iota(jnp.int32, (K, K), 1)
        self.w[...] = (r == c).astype(F32)

    def advance(self):
        b, start = self.B, self.block * self.B
        self.block += 1
        rows = pl.ds(start, b)
        pg, pu = self.g[rows, :], self.w[rows, :]
        sub = lax.broadcasted_iota(jnp.int32, (b, 1), 0)
        for j in range(b):
            col = pg[:, start + j : start + j + 1]
            p = col[j : j + 1, :]
            r = lax.rsqrt(p)
            r = r * (1.5 - 0.5 * p * r * r)
            f = jnp.where(sub > j, col * r, 0.0)
            sg, su = pg[j : j + 1, :] * r, pu[j : j + 1, :] * r
            pg = jnp.where(sub == j, sg, pg - f * sg)
            pu = jnp.where(sub == j, su, pu - f * su)
        self.w[rows, :] = pu
        if start + b < K:
            lane = lax.broadcasted_iota(jnp.int32, (b, K), 1)
            low = jnp.where(lane >= start + b, pg, 0.0)
            down = (((0,), (0,)), ((), ()))
            self.g[...] = self.g[...] - lax.dot_general(low, low, down, precision=HI, preferred_element_type=F32)
            self.w[...] = self.w[...] - lax.dot_general(low, pu, down, precision=HI, preferred_element_type=F32)


def gram(v):
    return lax.dot_general(v, v, (((0,), (0,)), ((), ())), precision=HI, preferred_element_type=F32)


def times_t(v, w):
    return lax.dot_general(v, w, (((1,), (1,)), ((), ())), precision=HI, preferred_element_type=F32)


def main_kernel(
    slot_ref, tiles_hbm, sketch_hbm,
    f_out, w_out, s_out, g_out,
    tiles, dense, sketch, part, ra0, ra1, ra2, ra3, rb0, rb1, rb2, rb3,
    blocks, xt, bp, sb, rc, sz0, sz1, rz0, rz1, bt,
    gm, gh, gr0, gr1, gr2, ga, gfull, gwork, winv,
    load_sem, send_sem, recv_sem,
):
    net = Net(send_sem, recv_sem)
    load_tiles = pltpu.make_async_copy(tiles_hbm, tiles.at[pl.ds(0, tiles_hbm.shape[0])], load_sem.at[0])
    load_sketch = pltpu.make_async_copy(sketch_hbm, sketch, load_sem.at[1])
    load_tiles.start()
    load_sketch.start()

    barrier = pltpu.get_barrier_semaphore()
    for n in range(1, 16):
        pl.semaphore_signal(barrier, inc=1, device_id=(net.row, (net.col + n) % 16), device_id_type=MESH)
    for n in range(1, 4):
        pl.semaphore_signal(barrier, inc=1, device_id=net.to(z=(net.z + n) % 4), device_id_type=MESH)
    pl.semaphore_signal(barrier, inc=1, device_id=net.to(core=1 - net.core), device_id_type=MESH)

    tiles[tiles_hbm.shape[0]] = jnp.zeros((TILE, TILE), BF16)
    load_tiles.wait()

    def place(i, _):
        for j in range(CB):
            dense[pl.ds(pl.multiple_of(i * TILE, TILE), TILE), pl.ds(j * TILE, TILE)] = tiles[slot_ref[i * CB + j]]
        return 0

    lax.fori_loop(0, RB, place, 0)
    load_sketch.wait()
    pl.semaphore_wait(barrier, 19)

    step = 512

    def product_one(n, _):
        m, k = n // 8, n % 8
        a = dense[pl.ds(pl.multiple_of(m * step, step), step), pl.ds(pl.multiple_of(k * step, step), step)]
        b = sketch[pl.ds(pl.multiple_of(k * step, step), step), :]
        value = jnp.dot(a, b, preferred_element_type=F32).reshape(4, 4, 32, K)
        part[m] = jnp.where(k == 0, value, part[m] + value)
        return 0

    lax.fori_loop(0, 32, product_one, 0)
    reduce_scatter(net, part, ra0, ra1, ra2, ra3)

    first = part[net.x, net.y].reshape(TILE, K)
    f_out[...] = first
    first_t = first.T
    high = first_t.astype(BF16)
    low = (first_t - high.astype(F32)).astype(BF16)
    for q in range(4):
        blocks[net.x, net.y, q, 0] = high[q * 64 : q * 64 + 64, :]
        blocks[net.x, net.y, q, 1] = low[q * 64 : q * 64 + 64, :]
    gather = Gather(net, blocks)
    gather.advance()
    gm[0] = gram(first)
    sums = [
        GramSum(net, gm.at[i], gh.at[i], gr0.at[i], gr1.at[i], gr2.at[i], ga.at[i], gfull.at[i]) for i in range(2)
    ]
    sums[0].advance()
    gather.advance()
    sums[0].advance()
    gather.advance()
    gather.advance()
    sums[0].advance()
    gather.advance()
    sums[0].advance()

    for n in range(16):
        xt[:, n * TILE : (n + 1) * TILE] = blocks[n // 4, n % 4].reshape(2 * K, TILE)

    def product_two(core):
        def body(n, _):
            p = n // 2 * 2 + core
            col = pl.multiple_of(p * 512 + n % 2 * 256, 256)
            value = jnp.dot(xt[...], dense[:, pl.ds(col, 256)], preferred_element_type=F32)
            value = jnp.sum(value.reshape(4, 2, 64, 256), axis=1).reshape(K, 256)
            bp[p, :, pl.ds(pl.multiple_of(n % 2 * 256, 256), 256)] = value
            return 0

        lax.fori_loop(0, 8, body, 0)

    other = net.to(core=1 - net.core)
    product_two(1 - net.core)
    copies = []
    for z in range(4):
        sb[z] = bp[2 * z + 1 - net.core].astype(BF16)
        copies.append(net.start(sb.at[z], rc.at[z], other))
    product_two(net.core)
    sums[0].advance()
    for z in range(4):
        copies[z].wait_recv()
        p = 2 * z + net.core
        bp[p] = bp[p] + rc[z].astype(F32)

    sums[0].advance()
    factor = Factor(gwork, winv)
    gwork[...] = gfull[0].reshape(K, K)
    factor.begin()

    half = K // 2
    edges = ((1, 3), (3, 1))
    zc = []
    for h, (e, g) in enumerate(edges):
        rows = pl.ds(h * half, half)
        to = net.to(z=flip(net.z, e))
        for i, k in enumerate((e, 2)):
            sz0[h, i] = bp[2 * flip(net.z, k) + net.core, rows, :].astype(BF16)
            zc.append(net.start(sz0.at[h, i], rz0.at[h, i], to))
    factor.advance()
    factor.advance()
    zd = []
    for h, (e, g) in enumerate(edges):
        rows = pl.ds(h * half, half)
        zc[2 * h + 1].wait_recv()
        p = 2 * flip(net.z, g) + net.core
        sz1[h] = (bp[p, rows, :] + rz0[h, 1].astype(F32)).astype(BF16)
        zd.append(net.start(sz1.at[h], rz1.at[h], net.to(z=flip(net.z, g))))
    factor.advance()
    ze = []
    for h, (e, g) in enumerate(edges):
        rows = pl.ds(h * half, half)
        zc[2 * h].wait_recv()
        zd[h].wait_recv()
        p = 2 * net.z + net.core
        value = bp[p, rows, :] + rz0[h, 0].astype(F32) + rz1[h].astype(F32)
        bt[net.z, net.core, h] = value.astype(BF16)
        ref = bt.at[net.z, net.core, h]
        ze.append(net.start(ref, ref, net.to(z=flip(net.z, e))))
    factor.advance()
    zf = []
    for h, (e, g) in enumerate(edges):
        ze[h].wait_recv()
        for z in (net.z, flip(net.z, e)):
            ref = bt.at[z, net.core, h]
            zf.append(net.start(ref, ref, net.to(z=flip(net.z, g))))
    factor.advance()
    factor.advance()
    for copy in zf:
        copy.wait_recv()
    last = net.start(bt.at[:, net.core], bt.at[:, net.core], other)
    factor.advance()
    factor.advance()
    w_out[...] = winv[...]
    last.wait_recv()

    net.close()

    def product_three(n, _):
        m, k = n // 8, n % 8
        a = dense[pl.ds(pl.multiple_of(m * step, step), step), pl.ds(pl.multiple_of(k * step, step), step)]
        b = bt[k // 2, k % 2].reshape(K, step)
        value = lax.dot_general(a, b, (((1,), (1,)), ((), ())), preferred_element_type=F32).reshape(4, 4, 32, K)
        part[m] = jnp.where(k == 0, value, part[m] + value)
        return 0

    lax.fori_loop(0, 32, product_three, 0)
    reduce_scatter(net, part, rb0, rb1, rb2, rb3)
    second = times_t(part[net.x, net.y].reshape(TILE, K), winv[...])
    s_out[...] = second
    gm[1] = gram(second)
    for _ in range(6):
        sums[1].advance()
    g_out[...] = gfull[1].reshape(K, K)
    net.close()


def last_kernel(scale, f_ref, w_ref, s_ref, g_ref, range_ref, basis_ref, gwork, winv):
    range_ref[...] = times_t(f_ref[...], w_ref[...]) * scale
    gwork[...] = g_ref[...]
    factor = Factor(gwork, winv)
    factor.begin()
    for _ in range(K // Factor.B):
        factor.advance()
    basis_ref[...] = times_t(s_ref[...], winv[...]) * scale


def body(tile_data, tile_rows, tile_cols, tile_count, sketch):
    tiles = tile_data[0, 0]
    total = tiles.shape[0]
    number = jnp.arange(total, dtype=jnp.int32)
    place = tile_rows[0, 0] * CB + tile_cols[0, 0]
    place = jnp.where(number < tile_count[0, 0], place, -1)
    hit = place[None, :] == jnp.arange(RB * CB, dtype=jnp.int32)[:, None]
    slot = jnp.min(jnp.where(hit, number[None, :], total), axis=1)
    vmem = pl.BlockSpec(memory_space=pltpu.VMEM)
    hbm = pl.BlockSpec(memory_space=pl.ANY)
    square = jax.ShapeDtypeStruct((K, K), F32)
    share = jax.ShapeDtypeStruct((TILE, K), F32)

    def stages(dtype):
        return [
            pltpu.VMEM((4, 2, 4, 32, K), dtype),
            pltpu.VMEM((4, 4, 32, K), dtype),
            pltpu.VMEM((4, 2, 32, K), dtype),
            pltpu.VMEM((4, 32, K), dtype),
        ]

    first, inverse, second, gram_two = pl.pallas_call(
        main_kernel,
        out_shape=(share, square, share, square),
        in_specs=[pl.BlockSpec(memory_space=pltpu.SMEM), hbm, hbm],
        out_specs=(vmem,) * 4,
        scratch_shapes=[
            pltpu.VMEM((total + 1, TILE, TILE), BF16),
            pltpu.VMEM((ROWS_DEV, COLS_DEV), BF16),
            pltpu.VMEM((COLS_DEV, K), BF16),
            pltpu.VMEM((4, 4, 4, 32, K), F32),
            *stages(F32),
            *stages(F32),
            pltpu.VMEM((4, 4, 4, 2, 64, TILE), BF16),
            pltpu.VMEM((2 * K, ROWS_DEV), BF16),
            pltpu.VMEM((8, K, 512), F32),
            pltpu.VMEM((4, K, 512), BF16),
            pltpu.VMEM((4, K, 512), BF16),
            pltpu.VMEM((2, 2, K // 2, 512), BF16),
            pltpu.VMEM((2, K // 2, 512), BF16),
            pltpu.VMEM((2, 2, K // 2, 512), BF16),
            pltpu.VMEM((2, K // 2, 512), BF16),
            pltpu.VMEM((4, 2, 2, K // 2, 512), BF16),
            pltpu.VMEM((2, K, K), F32),
            pltpu.VMEM((2, 16, 8, K), F32),
            pltpu.VMEM((2, K // 2, K), F32),
            pltpu.VMEM((2, 16, 8, K), F32),
            pltpu.VMEM((2, 4, 8, K), F32),
            pltpu.VMEM((2, 16, 8, K), F32),
            pltpu.VMEM((2, 2, 16, 8, K), F32),
            pltpu.VMEM((K, K), F32),
            pltpu.VMEM((K, K), F32),
            pltpu.SemaphoreType.DMA((2,)),
            pltpu.SemaphoreType.DMA((COPIES,)),
            pltpu.SemaphoreType.DMA((COPIES,)),
        ],
        compiler_params=pltpu.CompilerParams(
            collective_id=0, has_side_effects=True, vmem_limit_bytes=60 * 1024 * 1024
        ),
        name="range_finder",
    )(slot, tiles, sketch)
    scale = math.sqrt(ROWS_DEV * lax.axis_size("row"))
    return pl.pallas_call(
        lambda *refs: last_kernel(scale, *refs),
        out_shape=(share, share),
        in_specs=[vmem] * 4,
        out_specs=(vmem, vmem),
        scratch_shapes=[pltpu.VMEM((K, K), F32)] * 2,
        name="finish",
    )(first, inverse, second, gram_two)


def solution(mesh):
    placed = (
        P("row", "col", None, None, None),
        P("row", "col", None),
        P("row", "col", None),
        P("row", "col"),
        P("col", None),
    )
    return jax.shard_map(
        body,
        mesh=mesh,
        in_specs=placed,
        out_specs=(P(("row", "col"), None), P(("row", "col"), None)),
        check_vma=False,
    )
```

time: 1020 us -> 192 us (0.19); the launches traced: 1010 us -> 192 us
  waiting for transfers between devices: 481 us -> 0 us
  matrix products: 260 us -> 0 us
  Pallas kernels: 0 us -> 189 us
  other arithmetic: 122 us -> 1.44 us
  local copies, waits for them, and re-layouts: 69.3 us -> 0 us
  blocking collectives: 58.1 us -> 0 us
  between operations: 17 us -> 1.29 us
    psum x2 -> x0, waiting for transfers between devices: 293 us -> none  [the longest x1 147 us: body(): gram_two = lax.psum(gram_of(second_share), ('row', 'col'))]
    dot_general x28 -> x0, matrix products: 257 us -> none  [the longest x12 162 us: step(): jnp.einsum('nt,tak->nak', select, product, precision=lax.Precision.HIGHEST)]
    pallas_call x0 -> x2, Pallas kernels: none -> 189 us  [the longest x1 160 us: body(): pl.pallas_call(main_kernel, out_shape=(share, square, share, square), in_...]
    reduce_scatter x2 -> x0, waiting for transfers between devices: 150 us -> none  [the longest x1 76.8 us: body(): share = lax.psum_scatter(first, 'col', scatter_dimension=0, tiled=True)]
    another operation x18 -> x0, other arithmetic: 108 us -> none  [the longest x13 68.7 us: orthonormal(): lower = jnp.linalg.cholesky(gram)]
    psum x1 -> x0, blocking collectives: 58.1 us -> none  [body(): cross_full = lax.psum(cross, 'row').astype(jnp.bfloat16)]
    gather x12 -> x0, local copies, waits for them, and re-layouts: 44.7 us -> none  [step(): gathered = jnp.take(operand, source, axis=0)]
    all_gather x1 -> x0, waiting for transfers between devices: 38.1 us -> none  [body(): lax.all_gather(share_float.astype(jnp.bfloat16), 'col', axis=0, tiled=True)]
  transfers between devices with their start and end apart: 5 -> 0, of which waited for: 5 -> 0; matrix products, arithmetic and copies ran while one was open for 0% -> 0% of each run, Pallas kernels for 0% -> 0%
where the time goes in v1:
time: 192 us
  Pallas kernels  189 us (98%)
    pallas_call x1, Pallas kernels, body(): pl.pallas_call(main_kernel, out_shape=(share, square, share, square), in_...  160 us
    pallas_call x1, Pallas kernels, body(): pl.pallas_call(lambda *refs: last_kernel(scale, *refs), out_shape=(share,...  29 us

profile of v1, /device:TPU:1, one launch (start us, length us, event | category | flops | bytes accessed | tf_op | source)
XLA Modules:
  0.0 192.2 jit_solution(14432355948854686813)
XLA Ops:
  1.3 0.7 multiply_add_fusion
  2.0 0.7 select_reduce_fusion.slot_ref
  2.7 160.5 %range_finder.1 = (f32[128,256]{1,0:T(8,128)}, f32[256,256]{1,0:T(8,128)}, f32[128,256]{1,0:T(8,128)}, f32[256,256]{1,0:T(8,128)}) custom-call(s32[512]{0:T(512)} %select_reduce_fusion.slot_ref, bf16[256,128,128]{2,1,0:T(8,128)(2,1)} %bitcast.4, bf16[4096,256]{1,0:T(8,128)(2,1)} %sketch_hbm.1), custom_call_target="tpu_custom_call" | custom-call | tf_op jit(solution)/shard_map/range_finder/pallas_call | solution.py:420
  163.2 29.0 %finish.1 = (f32[128,256]{1,0:T(8,128)}, f32[128,256]{1,0:T(8,128)}) custom-call(f32[128,256]{1,0:T(8,128)} %get-tuple-element.6.refs_0_, f32[256,256]{1,0:T(8,128)} %get-tuple-element.7.refs_1_, f32[128,256]{1,0:T(8,128)} %get-tuple-element.8.refs_2_, f32[256,256]{1,0:T(8,128)} %get-tuple-element.9.refs_3_), custom_call_target="tpu_custom_call" | custom-call | tf_op jit(solution)/shard_map/finish/pallas_call | solution.py:461
  (1 shorter events, 0.0 us)

commit v2 on v1

v2 whole, which is shorter than its diff:
```python
import math

import jax
import jax.numpy as jnp
from jax import lax
from jax.experimental import pallas as pl
from jax.experimental.pallas import tpu as pltpu
from jax.sharding import PartitionSpec as P

MESH = pl.DeviceIdType.MESH
F32, BF16 = jnp.float32, jnp.bfloat16
HI = lax.Precision.HIGHEST
TILE, K, RB, CB = 128, 256, 16, 32
ROWS_DEV, COLS_DEV = RB * TILE, CB * TILE
COPIES = 208


def flip(c, e):
    return (c // 2 + e // 2) % 2 * 2 + (c + e) % 2


ORDERS = ((0, 1, 3), (0, 3, 1), (1, 1, 3), (1, 3, 1))
ALL = slice(None)


class Copy:
    def __init__(self, net, number, make):
        self.net, self.number, self.make = net, number, make

    def copy(self):
        src, dst, device = self.make()
        return pltpu.make_async_remote_copy(
            src_ref=src, dst_ref=dst, send_sem=self.net.send.at[self.number], recv_sem=self.net.recv.at[self.number],
            device_id=device, device_id_type=MESH,
        )

    def start(self):
        self.copy().start()
        return self

    def wait(self):
        self.copy().wait_recv()


class Net:
    def __init__(self, send, recv):
        self.send, self.recv, self.count = send, recv, 0
        self.open = []
        r, c = lax.axis_index("row"), lax.axis_index("col")
        self.z, self.core, self.x, self.y = r // 2, r % 2, c // 4, c % 4
        self.row, self.col = r, c
        self.pos = (self.x, self.y)

    def to(self, x=None, y=None, z=None, core=None):
        x = self.x if x is None else x
        y = self.y if y is None else y
        z = self.z if z is None else z
        core = self.core if core is None else core
        return (z * 2 + core, x * 4 + y)

    def peer(self, axis, e):
        return self.to(x=flip(self.x, e)) if axis == 0 else self.to(y=flip(self.y, e))

    def plan(self, make):
        copy = Copy(self, self.count, make)
        self.count += 1
        self.open.append(copy)
        return copy

    def family(self, n, make):
        base = self.count
        self.count += n
        self.open += [Copy(self, base + t, lambda t=t: make(t)) for t in range(n)]
        return lambda t: Copy(self, base + t, lambda: make(t))

    def start(self, make):
        return self.plan(make).start()

    def close(self):
        for copy in self.open:
            copy.copy().wait_send()
        self.open = []


def at2(ref, axis, a, b, *rest):
    return ref.at[(a, b, *rest)] if axis == 0 else ref.at[(b, a, *rest)]


def reduce_scatter(net, part, r0, r1, r2, r3, compute):
    def add(axis, a, b, q, value):
        ref = at2(part, axis, a, b, q)
        ref[...] = ref[...] + value

    first, across = {}, {}
    for q in (0, 1):
        _, e, g = ORDERS[q]
        for i, k in enumerate((e, 2)):
            first[q, i] = net.plan(
                lambda q=q, i=i, k=k, e=e: (part.at[flip(net.x, k), :, q], r0.at[q, i], net.peer(0, e))
            )
    for q in (2, 3):
        _, e, g = ORDERS[q]
        for i, k in enumerate((e, 2)):
            across[q, i] = net.family(
                4,
                lambda t, q=q, i=i, k=k, e=e: (
                    part.at[flip(net.x, (t + 1) % 4), flip(net.y, k), q],
                    r0.at[q, i, flip(net.x, (t + 1) % 4)],
                    net.peer(1, e),
                ),
            )

    def step(t, _):
        compute(flip(net.x, (t + 1) % 4))
        for key in across:
            across[key](t).start()
        for now, keys in ((0, [(0, 0)]), (1, [(0, 1), (1, 1)]), (2, [(1, 0)])):

            @pl.when(t == now)
            def _():
                for key in keys:
                    first[key].start()

        return 0

    lax.fori_loop(0, 4, step, 0)

    def wait_first(q, i):
        if q < 2:
            first[q, i].wait()
        else:
            for t in range(4):
                across[q, i](t).wait()

    second, third, fourth = {}, {}, {}
    for q, (axis, e, g) in enumerate(ORDERS):
        c = net.pos[axis]
        wait_first(q, 1)
        add(axis, flip(c, g), ALL, q, r0[q, 1])
        second[q] = net.start(
            lambda q=q, axis=axis, g=g: (at2(part, axis, flip(net.pos[axis], g), ALL, q), r1.at[q], net.peer(axis, g))
        )
        wait_first(q, 0)
        add(axis, c, ALL, q, r0[q, 0])
    for q, (axis, e, g) in enumerate(ORDERS):
        c, other = net.pos[axis], 1 - axis
        second[q].wait()
        add(axis, c, ALL, q, r1[q])
        for i, k in enumerate((e, 2)):
            third[q, i] = net.start(
                lambda q=q, i=i, k=k, axis=axis, other=other, e=e: (
                    at2(part, other, flip(net.pos[other], k), net.pos[axis], q), r2.at[q, i], net.peer(other, e)
                )
            )
    for q, (axis, e, g) in enumerate(ORDERS):
        c, d, other = net.pos[axis], net.pos[1 - axis], 1 - axis
        third[q, 1].wait()
        add(axis, c, flip(d, g), q, r2[q, 1])
        fourth[q] = net.start(
            lambda q=q, axis=axis, other=other, g=g: (
                at2(part, other, flip(net.pos[other], g), net.pos[axis], q), r3.at[q], net.peer(other, g)
            )
        )
        third[q, 0].wait()
        add(axis, c, d, q, r2[q, 0])
    for q, (axis, e, g) in enumerate(ORDERS):
        fourth[q].wait()
        add(axis, net.pos[axis], net.pos[1 - axis], q, r3[q])


class Gather:
    def __init__(self, net, buf):
        self.net, self.buf, self.step, self.flying = net, buf, 0, []

    def advance(self):
        net, buf, t = self.net, self.buf, self.step
        for copy in self.flying:
            copy.wait()
        self.flying = []
        self.step += 1
        if t == 4:
            return
        for q, (axis, e, g) in enumerate(ORDERS):
            other = 1 - axis
            link = ((axis, e), (axis, g), (other, e), (other, g))[t]
            moves = ((0, 0),) if t == 0 else ((0, 0), (e, 0)) if t == 1 else ((None, 0),) if t == 2 else ((None, 0), (None, e))
            for i, j in moves:

                def make(q=q, axis=axis, link=link, i=i, j=j):
                    a = ALL if i is None else flip(net.pos[axis], i)
                    ref = at2(buf, axis, a, flip(net.pos[1 - axis], j), q)
                    return ref, ref, net.peer(*link)

                self.flying.append(net.start(make))


class GramSum:
    def __init__(self, net, g, h, r0, r1, r2, ga, out):
        self.net, self.g, self.h, self.r0, self.r1, self.r2, self.ga, self.out = net, g, h, r0, r1, r2, ga, out
        self.phase, self.flying = 0, []

    def advance(self):
        net, half = self.net, K // 2
        for copy in self.flying:
            copy.wait()
        self.flying = []
        phase = self.phase
        self.phase += 1

        def rows(core):
            return pl.ds(pl.multiple_of(core * half, half), half)

        def send(make):
            self.flying.append(net.start(make))

        if phase == 0:
            send(lambda: (self.g.at[rows(1 - net.core)], self.r0, net.to(core=1 - net.core)))
        elif phase == 1:
            self.h[...] = (self.g[rows(net.core), :] + self.r0[...]).reshape(16, 8, K)
            for n in range(1, 16):
                send(lambda n=n: (self.h.at[(net.col + n) % 16], self.r1.at[n], (net.row, (net.col + n) % 16)))
            self.r1[0] = self.h[net.col]
        elif phase == 2:
            self.r2[net.z] = jnp.sum(self.r1[...], axis=0)
            for n in range(1, 4):
                send(lambda n=n: (self.r2.at[net.z], self.r2.at[net.z], net.to(z=(net.z + n) % 4)))
        elif phase == 3:
            self.ga[net.col] = jnp.sum(self.r2[...], axis=0)
            for n in range(1, 16):
                send(lambda n=n: (self.ga.at[net.col], self.ga.at[net.col], (net.row, (net.col + n) % 16)))
        elif phase == 4:
            self.out[net.core] = self.ga[...]
            send(lambda: (self.ga, self.out.at[net.core], net.to(core=1 - net.core)))


class Factor:
    B, S = 64, 8

    def __init__(self, g, w):
        self.g, self.w, self.block = g, w, 0

    def begin(self):
        r = lax.broadcasted_iota(jnp.int32, (K, K), 0)
        c = lax.broadcasted_iota(jnp.int32, (K, K), 1)
        self.w[...] = (r == c).astype(F32)

    def advance(self):
        b, start = self.B, self.block * self.B
        self.block += 1
        rows = pl.ds(start, b)
        pg, pu = self.g[rows, :], self.w[rows, :]
        sub = lax.broadcasted_iota(jnp.int32, (b, 1), 0)
        wide = lax.broadcasted_iota(jnp.int32, (b, 128), 0)
        for s in range(0, b, self.S):
            at = start + s
            cols = [jnp.broadcast_to(pg[:, at + k : at + k + 1], (b, 128)) for k in range(self.S)]
            factors, roots = [], []
            for k in range(self.S):
                p = cols[k][s + k : s + k + 1, :]
                r = lax.rsqrt(p)
                r = r * (1.5 - 0.5 * p * r * r)
                f = cols[k] * r
                for m in range(k + 1, self.S):
                    cols[m] = cols[m] - f * f[s + m : s + m + 1, :]
                factors.append(jnp.where(wide > s + k, f, 0.0))
                roots.append(r)
            for k in range(self.S):
                r = jnp.concatenate([roots[k], roots[k]], axis=1)
                f = jnp.concatenate([factors[k], factors[k]], axis=1)
                sg, su = pg[s + k : s + k + 1, :] * r, pu[s + k : s + k + 1, :] * r
                pg = jnp.where(sub == s + k, sg, pg - f * sg)
                pu = jnp.where(sub == s + k, su, pu - f * su)
        self.w[rows, :] = pu
        if start + b < K:
            lane = lax.broadcasted_iota(jnp.int32, (b, K), 1)
            low = jnp.where(lane >= start + b, pg, 0.0)
            down = (((0,), (0,)), ((), ()))
            self.g[...] = self.g[...] - lax.dot_general(low, low, down, precision=HI, preferred_element_type=F32)
            self.w[...] = self.w[...] - lax.dot_general(low, pu, down, precision=HI, preferred_element_type=F32)


def gram(v):
    return lax.dot_general(v, v, (((0,), (0,)), ((), ())), precision=HI, preferred_element_type=F32)


def times_t(v, w):
    return lax.dot_general(v, w, (((1,), (1,)), ((), ())), precision=HI, preferred_element_type=F32)


def main_kernel(
    slot_ref, tiles_hbm, sketch_hbm,
    f_out, w_out, s_out, g_out,
    tiles, dense, sketch, part, ra0, ra1, ra2, ra3, rb0, rb1, rb2, rb3,
    blocks, xt, bp, sb, rc, sz0, sz1, rz0, rz1, bt,
    gm, gh, gr0, gr1, gr2, ga, gfull, gwork, winv,
    load_sem, send_sem, recv_sem,
):
    net = Net(send_sem, recv_sem)
    load_tiles = pltpu.make_async_copy(tiles_hbm, tiles.at[pl.ds(0, tiles_hbm.shape[0])], load_sem.at[0])
    load_sketch = pltpu.make_async_copy(sketch_hbm, sketch, load_sem.at[1])
    load_tiles.start()
    load_sketch.start()

    barrier = pltpu.get_barrier_semaphore()
    for n in range(1, 16):
        pl.semaphore_signal(barrier, inc=1, device_id=(net.row, (net.col + n) % 16), device_id_type=MESH)
    for n in range(1, 4):
        pl.semaphore_signal(barrier, inc=1, device_id=net.to(z=(net.z + n) % 4), device_id_type=MESH)
    pl.semaphore_signal(barrier, inc=1, device_id=net.to(core=1 - net.core), device_id_type=MESH)

    tiles[tiles_hbm.shape[0]] = jnp.zeros((TILE, TILE), BF16)
    load_tiles.wait()

    def place(i, _):
        for j in range(CB):
            dense[pl.ds(pl.multiple_of(i * TILE, TILE), TILE), pl.ds(j * TILE, TILE)] = tiles[slot_ref[i * CB + j]]
        return 0

    lax.fori_loop(0, RB, place, 0)
    load_sketch.wait()
    pl.semaphore_wait(barrier, 19)

    step = 512

    def rows_of(m):
        return pl.ds(pl.multiple_of(m * step, step), step)

    def product_one(m):
        part[m] = jnp.dot(dense[rows_of(m), :], sketch[...], preferred_element_type=F32).reshape(4, 4, 32, K)

    reduce_scatter(net, part, ra0, ra1, ra2, ra3, product_one)

    first = part[net.x, net.y].reshape(TILE, K)
    f_out[...] = first
    first_t = first.T
    high = first_t.astype(BF16)
    low = (first_t - high.astype(F32)).astype(BF16)
    for q in range(4):
        blocks[net.x, net.y, q, 0] = high[q * 64 : q * 64 + 64, :]
        blocks[net.x, net.y, q, 1] = low[q * 64 : q * 64 + 64, :]
    gather = Gather(net, blocks)
    sums = [
        GramSum(net, gm.at[i], gh.at[i], gr0.at[i], gr1.at[i], gr2.at[i], ga.at[i], gfull.at[i]) for i in range(2)
    ]
    gather.advance()
    gm[0] = gram(first)
    sums[0].advance()
    gather.advance()
    gather.advance()
    sums[0].advance()
    gather.advance()
    gather.advance()

    for n in range(16):
        xt[:, n * TILE : (n + 1) * TILE] = blocks[n // 4, n % 4].reshape(2 * K, TILE)

    half = K // 2
    edges = ((1, 3), (3, 1))

    def piece(z, core):
        return pl.ds(pl.multiple_of((2 * z + core) * step, step), step)

    def product_two(z, core):
        value = jnp.dot(xt[...], dense[:, piece(z, core)], preferred_element_type=F32)
        return jnp.sum(value.reshape(4, 2, 64, step), axis=1).reshape(K, step)

    def z_of(t):
        return flip(net.z, (t + 1) % 4)

    swap = net.family(4, lambda t: (sb.at[z_of(t)], rc.at[z_of(t)], net.to(core=1 - net.core)))
    zc = {
        (h, i): net.plan(lambda h=h, i=i, e=e: (sz0.at[h, i], rz0.at[h, i], net.to(z=flip(net.z, e))))
        for h, (e, g) in enumerate(edges)
        for i in range(2)
    }

    def cross_step(t, _):
        z = z_of(t)
        sb[z] = product_two(z, 1 - net.core).astype(BF16)
        swap(t).start()
        bp[z] = product_two(z, net.core)
        swap(t).wait()
        bp[z] = bp[z] + rc[z].astype(F32)
        for now, keys in ((0, [(0, 0)]), (1, [(0, 1), (1, 1)]), (2, [(1, 0)])):

            @pl.when(t == now)
            def _():
                for h, i in keys:
                    sz0[h, i] = bp[z, h * half : (h + 1) * half, :].astype(BF16)
                    zc[h, i].start()

        return 0

    lax.fori_loop(0, 2, cross_step, 0)
    sums[0].advance()
    lax.fori_loop(2, 4, cross_step, 0)
    sums[0].advance()

    zd = []
    for h, (e, g) in enumerate(edges):
        zc[h, 1].wait()
        sz1[h] = (bp[flip(net.z, g), h * half : (h + 1) * half, :] + rz0[h, 1].astype(F32)).astype(BF16)
        zd.append(net.start(lambda h=h, g=g: (sz1.at[h], rz1.at[h], net.to(z=flip(net.z, g)))))
    sums[0].advance()

    def bt_at(z, core, h):
        return bt.at[pl.ds(h * half, half), piece(z, core)]

    ze = []
    for h, (e, g) in enumerate(edges):
        zc[h, 0].wait()
        zd[h].wait()
        value = bp[net.z, h * half : (h + 1) * half, :] + rz0[h, 0].astype(F32) + rz1[h].astype(F32)
        bt[pl.ds(h * half, half), piece(net.z, net.core)] = value.astype(BF16)

        def make(h=h, e=e):
            ref = bt_at(net.z, net.core, h)
            return ref, ref, net.to(z=flip(net.z, e))

        ze.append(net.start(make))
    sums[0].advance()
    factor = Factor(gwork, winv)
    gwork[...] = gfull[0].reshape(K, K)
    factor.begin()
    factor.advance()
    zf = []
    for h, (e, g) in enumerate(edges):
        ze[h].wait()
        for k in (0, e):

            def make(h=h, g=g, k=k):
                ref = bt_at(flip(net.z, k), net.core, h)
                return ref, ref, net.to(z=flip(net.z, g))

            zf.append(net.start(make))
    factor.advance()
    factor.advance()
    for copy in zf:
        copy.wait()
    last = []
    for z in range(4):

        def make(z=z):
            ref = bt.at[:, piece(z, net.core)]
            return ref, ref, net.to(core=1 - net.core)

        last.append(net.start(make))
    factor.advance()
    w_out[...] = winv[...]
    for copy in last:
        copy.wait()

    net.close()

    def product_three(m):
        value = lax.dot_general(dense[rows_of(m), :], bt[...], (((1,), (1,)), ((), ())), preferred_element_type=F32)
        part[m] = value.reshape(4, 4, 32, K)

    reduce_scatter(net, part, rb0, rb1, rb2, rb3, product_three)
    second = times_t(part[net.x, net.y].reshape(TILE, K), winv[...])
    s_out[...] = second
    gm[1] = gram(second)
    for _ in range(6):
        sums[1].advance()
    g_out[...] = gfull[1].reshape(K, K)
    net.close()


def last_kernel(scale, f_ref, w_ref, s_ref, g_ref, range_ref, basis_ref, gwork, winv):
    range_ref[...] = times_t(f_ref[...], w_ref[...]) * scale
    gwork[...] = g_ref[...]
    factor = Factor(gwork, winv)
    factor.begin()
    for _ in range(K // Factor.B):
        factor.advance()
    basis_ref[...] = times_t(s_ref[...], winv[...]) * scale


def body(tile_data, tile_rows, tile_cols, tile_count, sketch):
    tiles = tile_data[0, 0]
    total = tiles.shape[0]
    number = jnp.arange(total, dtype=jnp.int32)
    place = tile_rows[0, 0] * CB + tile_cols[0, 0]
    place = jnp.where(number < tile_count[0, 0], place, -1)
    hit = place[None, :] == jnp.arange(RB * CB, dtype=jnp.int32)[:, None]
    slot = jnp.min(jnp.where(hit, number[None, :], total), axis=1)
    vmem = pl.BlockSpec(memory_space=pltpu.VMEM)
    hbm = pl.BlockSpec(memory_space=pl.ANY)
    square = jax.ShapeDtypeStruct((K, K), F32)
    share = jax.ShapeDtypeStruct((TILE, K), F32)

    def stages(dtype):
        return [
            pltpu.VMEM((4, 2, 4, 32, K), dtype),
            pltpu.VMEM((4, 4, 32, K), dtype),
            pltpu.VMEM((4, 2, 32, K), dtype),
            pltpu.VMEM((4, 32, K), dtype),
        ]

    first, inverse, second, gram_two = pl.pallas_call(
        main_kernel,
        out_shape=(share, square, share, square),
        in_specs=[pl.BlockSpec(memory_space=pltpu.SMEM), hbm, hbm],
        out_specs=(vmem,) * 4,
        scratch_shapes=[
            pltpu.VMEM((total + 1, TILE, TILE), BF16),
            pltpu.VMEM((ROWS_DEV, COLS_DEV), BF16),
            pltpu.VMEM((COLS_DEV, K), BF16),
            pltpu.VMEM((4, 4, 4, 32, K), F32),
            *stages(F32),
            *stages(F32),
            pltpu.VMEM((4, 4, 4, 2, 64, TILE), BF16),
            pltpu.VMEM((2 * K, ROWS_DEV), BF16),
            pltpu.VMEM((4, K, 512), F32),
            pltpu.VMEM((4, K, 512), BF16),
            pltpu.VMEM((4, K, 512), BF16),
            pltpu.VMEM((2, 2, K // 2, 512), BF16),
            pltpu.VMEM((2, K // 2, 512), BF16),
            pltpu.VMEM((2, 2, K // 2, 512), BF16),
            pltpu.VMEM((2, K // 2, 512), BF16),
            pltpu.VMEM((K, COLS_DEV), BF16),
            pltpu.VMEM((2, K, K), F32),
            pltpu.VMEM((2, 16, 8, K), F32),
            pltpu.VMEM((2, K // 2, K), F32),
            pltpu.VMEM((2, 16, 8, K), F32),
            pltpu.VMEM((2, 4, 8, K), F32),
            pltpu.VMEM((2, 16, 8, K), F32),
            pltpu.VMEM((2, 2, 16, 8, K), F32),
            pltpu.VMEM((K, K), F32),
            pltpu.VMEM((K, K), F32),
            pltpu.SemaphoreType.DMA((2,)),
            pltpu.SemaphoreType.DMA((COPIES,)),
            pltpu.SemaphoreType.DMA((COPIES,)),
        ],
        compiler_params=pltpu.CompilerParams(
            collective_id=0, has_side_effects=True, vmem_limit_bytes=60 * 1024 * 1024
        ),
        name="range_finder",
    )(slot, tiles, sketch)
    scale = math.sqrt(ROWS_DEV * lax.axis_size("row"))
    return pl.pallas_call(
        lambda *refs: last_kernel(scale, *refs),
        out_shape=(share, share),
        in_specs=[vmem] * 4,
        out_specs=(vmem, vmem),
        scratch_shapes=[pltpu.VMEM((K, K), F32)] * 2,
        name="finish",
    )(first, inverse, second, gram_two)


def solution(mesh):
    placed = (
        P("row", "col", None, None, None),
        P("row", "col", None),
        P("row", "col", None),
        P("row", "col"),
        P("col", None),
    )
    return jax.shard_map(
        body,
        mesh=mesh,
        in_specs=placed,
        out_specs=(P(("row", "col"), None), P(("row", "col"), None)),
        check_vma=False,
    )
```

time: 192 us -> 148 us (0.77)
  Pallas kernels: 189 us -> 145 us
    pallas_call x1, Pallas kernels: 160 us -> 134 us  [body(): pl.pallas_call(main_kernel, out_shape=(share, square, share, square), in_...]
    pallas_call x1, Pallas kernels: 29 us -> 11.1 us  [body(): pl.pallas_call(lambda *refs: last_kernel(scale, *refs), out_shape=(share,...]
where the time goes in v2:
time: 148 us; the launch traced here: 147 us
  Pallas kernels  145 us (98%)
    pallas_call x1, Pallas kernels, body(): pl.pallas_call(main_kernel, out_shape=(share, square, share, square), in_...  134 us
    pallas_call x1, Pallas kernels, body(): pl.pallas_call(lambda *refs: last_kernel(scale, *refs), out_shape=(share,...  11.1 us

profile of v2, /device:TPU:1, one launch (start us, length us, event | category | flops | bytes accessed | tf_op | source)
XLA Modules:
  0.0 147.4 jit_solution(16076254960628794236)
XLA Ops:
  1.3 0.7 multiply_add_fusion
  2.0 0.7 select_reduce_fusion.slot_ref
  2.7 133.5 %range_finder.1 = (f32[128,256]{1,0:T(8,128)}, f32[256,256]{1,0:T(8,128)}, f32[128,256]{1,0:T(8,128)}, f32[256,256]{1,0:T(8,128)}) custom-call(s32[512]{0:T(512)} %select_reduce_fusion.slot_ref, bf16[256,128,128]{2,1,0:T(8,128)(2,1)} %bitcast.4, bf16[4096,256]{1,0:T(8,128)(2,1)} %sketch_hbm.1), custom_call_target="tpu_custom_call" | custom-call | tf_op jit(solution)/shard_map/range_finder/pallas_call | solution.py:500
  136.2 11.1 %finish.1 = (f32[128,256]{1,0:T(8,128)}, f32[128,256]{1,0:T(8,128)}) custom-call(f32[128,256]{1,0:T(8,128)} %get-tuple-element.6.refs_0_, f32[256,256]{1,0:T(8,128)} %get-tuple-element.7.refs_1_, f32[128,256]{1,0:T(8,128)} %get-tuple-element.8.refs_2_, f32[256,256]{1,0:T(8,128)} %get-tuple-element.9.refs_3_), custom_call_target="tpu_custom_call" | custom-call | tf_op jit(solution)/shard_map/finish/pallas_call | solution.py:541
  (1 shorter events, 0.0 us)
